TPU v7x, 32 devices: a whole 2x2x4 slice. The times are simulated.
32 devices in a mesh: dp: 8 (over z, x), seq: 4 (over y, core).
Axes of the slice: x: 2, y: 2, z: 4, core: 2. Of those that a mesh axis runs over, the one named last changes fastest.
Arguments:
- query: bfloat16 [8, 1024, 2048], P('dp', 'seq'), may hold values from -6 to 6
- keys: bfloat16 [8, 1024, 256], P('dp', 'seq'), may hold values from -6 to 6
- values: bfloat16 [8, 1024, 256], P('dp', 'seq'), may hold values from -6 to 6
- grad_out: bfloat16 [8, 1024, 2048], P('dp', 'seq'), may hold values from -6 to 6
- layer_input: bfloat16 [8, 1024, 1536], P('dp', 'seq'), may hold values from -6 to 6
- sinks: float32 [32], replicated, may hold values from 1 to 5
- segments: int32 [8, 1024], P('dp', 'seq'), may hold values from 0 to 255, as said below
- positions: int32 [8, 1024], P('dp', 'seq'), may hold values from 0 to 8191, as said below
Outputs:
- grad_query: bfloat16 [8, 1024, 2048], P('dp', 'seq')
- weight_grads: float32 [1536, 256], P('dp')
Inputs may be any that keep to these rules, and one draw needn't show every extreme that they name: `segments`: segment ids never fall along a span. positions rise by one inside a document.
All inputs are finite; a program needn't handle non-finite values.
Results may differ from a plain program's by a relative error of at most 0.0086.
Values may be sent and summed in bfloat16 or wider, within the bound.
No kernel may reach another device: no remote copies, remote signals or barrier semaphores. Data moves between devices by JAX's collectives and lax.ppermute only.
A program may use at most 64 MiB of HBM per device.

v0:
```python
import jax
import jax.numpy as jnp
from jax import lax
from jax.sharding import PartitionSpec as P

HEADDIM = 64
WINDOW = 128
theta_base = 150000.0
seg_modulus = 256


def from_behind(shard, axis, by):
    count = lax.axis_size(axis)
    pairs = [(i, i + by) for i in range(count) if 0 <= i + by < count]
    return lax.ppermute(shard, axis, pairs)


def rotate_back(grads, token_pos):
    half_dim = grads.shape[-1] // 2
    frequency = theta_base ** (-(jnp.arange(half_dim, dtype=jnp.float32) * 2.0 / grads.shape[-1]))
    angles = token_pos.astype(jnp.float32)[:, None] * frequency[None, :]
    cosine = jnp.cos(angles)[:, None, :]
    sine_val = jnp.sin(angles)[:, None, :]
    lower_half = grads[..., :half_dim]
    upper_half = grads[..., half_dim:]
    return jnp.concatenate(
        [lower_half * cosine + upper_half * sine_val, upper_half * cosine - lower_half * sine_val],
        axis=-1,
    )


def body(query, keys, values, grad_out, layer_input, sinks, segments, positions):
    query = query[0]
    keys = keys[0]
    values = values[0]
    grad_out = grad_out[0]
    layer_input = layer_input[0]
    segments = segments[0]
    positions = positions[0]
    tok_rows = query.shape[0]
    head_dim = HEADDIM
    heads_q = sinks.shape[0]
    heads_kv = keys.shape[1] // head_dim
    group = heads_q // heads_kv
    width = WINDOW
    scale = 1.0 / head_dim**0.5
    seg_local = jnp.remainder(segments, seg_modulus).astype(jnp.float32)
    rim_keys, rim_values, rim_segs = from_behind(
        (
            keys[tok_rows - width :],
            values[tok_rows - width :],
            seg_local[tok_rows - width :].astype(jnp.bfloat16),
        ),
        "seq",
        1,
    )
    all_keys = jnp.concatenate([rim_keys, keys], axis=0)
    all_values = jnp.concatenate([rim_values, values], axis=0)
    key_segs = jnp.concatenate([rim_segs.astype(jnp.float32), seg_local], axis=0)
    seq_index = lax.axis_index("seq")
    query_idx = jnp.arange(tok_rows)[:, None] + width
    key_idx = jnp.arange(tok_rows + width)[None, :]
    offset = query_idx - key_idx
    allowed = (offset >= 0) & (offset < width) & (seg_local[:, None] == key_segs[None, :])
    allowed = allowed & ((key_idx >= width) | (seq_index > 0))
    allowed = allowed[None]
    query_parts = []
    key_parts = []
    for head_group in range(heads_kv):
        low_col = head_group * group * head_dim
        high_col = low_col + group * head_dim
        q_grp = query[:, low_col:high_col].reshape(tok_rows, group, head_dim)
        g_grp = grad_out[:, low_col:high_col].reshape(tok_rows, group, head_dim)
        k_grp = all_keys[:, head_group * head_dim : (head_group + 1) * head_dim]
        v_grp = all_values[:, head_group * head_dim : (head_group + 1) * head_dim]
        scores = jnp.einsum("qhd,kd->hqk", q_grp, k_grp, preferred_element_type=jnp.float32) * scale
        sink_col = sinks[head_group * group : (head_group + 1) * group][:, None, None]
        masked = jnp.where(allowed, scores, -jnp.inf)
        peak = jnp.maximum(jnp.max(masked, axis=-1, keepdims=True), sink_col)
        expo = jnp.where(allowed, jnp.exp(masked - peak), 0.0)
        total = jnp.sum(expo, axis=-1, keepdims=True) + jnp.exp(sink_col - peak)
        probs = expo / total
        grad_probs = jnp.einsum("qhd,kd->hqk", g_grp, v_grp, preferred_element_type=jnp.float32)
        delta = jnp.sum(probs * grad_probs, axis=-1, keepdims=True)
        grad_scores = probs * (grad_probs - delta)
        grad_b = grad_scores.astype(jnp.bfloat16)
        grad_q = (
            jnp.einsum("hqk,kd->qhd", grad_b, k_grp, preferred_element_type=jnp.float32) * scale
        )
        query_parts.append(grad_q.reshape(tok_rows, group * head_dim).astype(jnp.bfloat16))
        key_parts.append(
            jnp.einsum("hqk,qhd->kd", grad_b, q_grp, preferred_element_type=jnp.float32) * scale
        )
    grad_query = jnp.concatenate(query_parts, axis=-1)
    key_grads = jnp.concatenate(key_parts, axis=-1)
    back_keys = from_behind(key_grads[:width].astype(jnp.bfloat16), "seq", -1).astype(jnp.float32)
    local_keys = key_grads[width:]
    local_keys = jnp.concatenate(
        [local_keys[: tok_rows - width], local_keys[tok_rows - width :] + back_keys], axis=0
    )
    turned = rotate_back(local_keys.reshape(tok_rows, heads_kv, head_dim), positions)
    k_grads = turned.reshape(tok_rows, heads_kv * head_dim).astype(jnp.bfloat16)
    shard = lax.psum_scatter(
        lax.dot_general(
            layer_input, k_grads, (((0,), (0,)), ((), ())), preferred_element_type=jnp.float32
        ),
        "dp",
        scatter_dimension=0,
        tiled=True,
    )
    shard = lax.psum(shard, "seq")
    return (grad_query[None], shard)


def solution(mesh):
    return jax.shard_map(
        body,
        mesh=mesh,
        in_specs=(
            P("dp", "seq", None),
            P("dp", "seq", None),
            P("dp", "seq", None),
            P("dp", "seq", None),
            P("dp", "seq", None),
            P(),
            P("dp", "seq"),
            P("dp", "seq"),
        ),
        out_specs=(P("dp", "seq", None), P("dp", None)),
        check_vma=False,
    )
```

profile of v0, /device:TPU:0, one launch (start us, length us, event | category | flops | bytes accessed | tf_op | source)
XLA Modules:
  0.0 173.2 jit_solution(16358544082177896071)
XLA Ops:
  7.2 0.8 fusion.83
  8.0 0.6 slice.98
  8.6 2.9 %collective-permute-start.1 = (bf16[128]{0:T(256)(128)(2,1)}, bf16[128]{0:T(256)(128)(2,1)}, u32[]{:S(2)}, u32[]{:S(2)}) collective-permute-start(bf16[128]{0:T(256)(128)(2,1)} %slice.98), channel_id=1, source_target_pairs={{0,1},{1,2},{2,3},{4,5},{5,6},{6,7},{8,9},{9,10},{10,11},{12,13},{... | collective-permute-start | bytes 776 | tf_op jit(solution)/shard_map/ppermute | solution.py:15
  11.5 1.0 copy.35
  12.5 0.6 slice_bitcast_fusion.1
  13.2 4.0 %collective-permute-start = (bf16[128,256]{0,1:T(8,128)(2,1)}, bf16[128,256]{0,1:T(8,128)(2,1)S(1)}, u32[]{:S(2)}, u32[]{:S(2)}) collective-permute-start(bf16[128,256]{0,1:T(8,128)(2,1)} %slice_bitcast_fusion.1), channel_id=1, source_target_pairs={{0,1},{1,2},{2,3},{4,5},{5,6},{6,7},{8,9},{9,10},{10,11},{12,13},{... | collective-permute-start | bytes 196616 | tf_op jit(solution)/shard_map/ppermute | solution.py:15
  17.2 1.0 copy.38
  18.2 0.6 slice_bitcast_fusion
  18.8 1.9 %collective-permute-start.2 = (bf16[128,256]{0,1:T(8,128)(2,1)}, bf16[128,256]{0,1:T(8,128)(2,1)S(1)}, u32[]{:S(2)}, u32[]{:S(2)}) collective-permute-start(bf16[128,256]{0,1:T(8,128)(2,1)} %slice_bitcast_fusion), channel_id=1, source_target_pairs={{0,1},{1,2},{2,3},{4,5},{5,6},{6,7},{8,9},{9,10},{10,11},{12,13},{... | collective-permute-start | bytes 196616 | tf_op jit(solution)/shard_map/ppermute | solution.py:15
  20.7 0.6 negate_power_fusion
  21.3 0.5 iota_add_fusion
  21.9 0.6 fusion.70
  22.4 1.2 convert_element_type.102
  23.7 1.3 fusion.88
  25.0 1.3 fusion.85
  26.3 0.1 copy.48
  26.4 0.1 copy.45
  26.6 0.1 copy.42
  26.7 0.1 copy.37
  26.9 0.9 fusion.86
  27.8 1.1 copy.40
  28.8 1.8 %copy.49 = bf16[256,512]{0,1:T(8,128)(2,1)} copy(bf16[256,512]{1,0:T(8,128)(2,1)} %get-tuple-element.22) | data formatting | bytes 524288 | tf_op jit(solution)/shard_map/slice | solution.py:73
  30.6 1.8 %copy.46 = bf16[256,512]{0,1:T(8,128)(2,1)} copy(bf16[256,512]{1,0:T(8,128)(2,1)} %get-tuple-element.23) | data formatting | bytes 524288 | tf_op jit(solution)/shard_map/slice | solution.py:73
  32.4 0.8 copy.43
  33.3 0.6 convert_element_type.84
  33.9 0.9 fusion.37
  34.8 0.6 fusion.89
  35.4 0.7 fusion.12
  36.1 0.8 fusion.17
  36.9 0.6 fusion.62
  37.5 0.6 fusion.68
  38.1 0.1 exponential_add_fusion.3
  38.1 2.5 %fusion.9 = (f32[8,256]{1,0:T(8,128)S(1)}, f32[8,256]{1,0:T(8,128)S(1)}, f32[8,256]{1,0:T(8,128)S(1)}, f32[8,256]{1,0:T(8,128)S(1)}, f32[384,256,8]{1,0,2:T(8,128)S(1)}) fusion(f32[8,256]{1,0:T(8,128)S(1)} %exponential_add_fusion.3, f32[8,256]{1,0:T(8,128)S(1)} %broadcast_maximum_fusion.3, f32[384,256,8]{1,0,2:T(8,128)S(1)} %get-tuple-element.41, ...), kind=kOutput, calls=%fused_computation.20 | convolution fusion | flops 113336320 | bytes 16334848 | tf_op jit(solution)/shard_map/qhd,kd->hqk/dot_general | solution.py:83
  40.7 2.0 %fusion.11 = (bf16[8,256,384]{1,2,0:T(8,128)(2,1)S(1)}, f32[8,256]{1,0:T(8,128)S(1)}) fusion(f32[384,256,8]{1,0,2:T(8,128)S(1)} %get-tuple-element.42, f32[8,256]{1,0:T(8,128)S(1)} %get-tuple-element.6, f32[8,256]{1,0:T(8,128)S(1)} %exponential_add_fusion.3, f32[8,256]{1,0:T(8,128)S(1)} %broadcast_maximum_fusion.3, f32[384,256,8]{1,0,2:T(8,128)S(1)} %get-tuple-element.41, ...), kind=kLoop, calls=%fused_computation.22 | loop fusion | flops 10221568 | bytes 11149312 | tf_op jit(solution)/shard_map/convert_element_type | solution.py:86
  42.7 0.6 fusion.31
  43.3 0.1 exponential_add_fusion.2
  43.5 2.8 %fusion.6 = (f32[8,256]{1,0:T(8,128)S(1)}, f32[8,256]{1,0:T(8,128)S(1)}, f32[8,256]{1,0:T(8,128)S(1)}, f32[384,256,8]{1,0,2:T(8,128)S(1)}) fusion(f32[8,256]{1,0:T(8,128)S(1)} %exponential_add_fusion.2, f32[8,256]{1,0:T(8,128)S(1)} %broadcast_maximum_fusion.2, f32[384,256,8]{1,0,2:T(8,128)S(1)} %fusion.62, pred[256,384]{0,1:T(8,128)(4,1)S(1)} %fusion.37, ...), kind=kOutput, calls=%fused_computation.14 | convolution fusion | flops 114124800 | bytes 13197312 | tf_op jit(solution)/shard_map/qhd,kd->hqk/dot_general | solution.py:83
  46.3 0.1 exponential_add_fusion
  46.4 0.6 fusion.57
  47.0 0.3 copy-done.10
  47.2 2.2 %fusion.3 = (f32[8,256]{1,0:T(8,128)S(1)}, f32[8,256]{1,0:T(8,128)S(1)}, f32[384,256,8]{1,0,2:T(8,128)S(1)}) fusion(f32[8,256]{1,0:T(8,128)S(1)} %get-tuple-element.46, f32[8,256]{1,0:T(8,128)S(1)} %broadcast_maximum_fusion.1, f32[384,256,8]{1,0,2:T(8,128)S(1)} %fusion.68, pred[256,384]{0,1:T(8,128)(4,1)S(1)} %fusion.37, f32[384,256,8]{1,0,2:T(8,128)S(1)} %fusion.57, ...), kind=kOutput, calls=%fused_computation.8 | convolution fusion | flops 111767552 | bytes 13189120 | tf_op jit(solution)/shard_map/qhd,kd->hqk/dot_general | solution.py:83
  49.5 3.6 %fusion.8 = (bf16[8,256,384]{1,2,0:T(8,128)(2,1)S(1)}, bf16[8,256,384]{1,2,0:T(8,128)(2,1)S(1)}, bf16[8,256,384]{1,2,0:T(8,128)(2,1)S(1)}) fusion(f32[384,256,8]{1,0,2:T(8,128)S(1)} %get-tuple-element.43, f32[8,256]{1,0:T(8,128)S(1)} %get-tuple-element.10, f32[8,256]{1,0:T(8,128)S(1)} %exponential_add_fusion.2, f32[8,256]{1,0:T(8,128)S(1)} %broadcast_maximum_fusion.2, ...), kind=kLoop, calls=%fused_computation.16 | loop fusion | flops 18874368 | bytes 23764992 | tf_op jit(solution)/shard_map/convert_element_type | solution.py:86
  53.2 0.6 fusion.29
  53.8 0.6 fusion.28
  54.4 0.6 fusion.30
  55.0 0.2 copy-done.4
  55.3 1.3 collective-permute-start.3
  56.6 0.2 multiply_cosine_fusion
  56.8 1.6 collective-permute-done.3
  58.5 1.5 convolution_bitcast_fusion
  60.1 3.1 %copy.68 = f32[1536,256]{1,0:T(8,128)} copy(f32[1536,256]{0,1:T(8,128)} %convolution_bitcast_fusion) | data formatting | bytes 3145728
  63.2 0.4 fusion.24
  63.6 0.1 copy.51
  63.7 1.9 %fusion.26 = bf16[64,8,256]{2,0,1:T(8,128)(2,1)S(1)} fusion(bf16[8,256,384]{1,2,0:T(8,128)(2,1)} %copy-done.4, bf16[256,256]{0,1:T(8,128)(2,1)S(1)} %bitcast.210, bf16[128,256]{0,1:T(8,128)(2,1)S(1)} %collective-permute-done), kind=kOutput, calls=%fused_computation.47 | convolution fusion | flops 101023744 | bytes 2031616 | tf_op jit(solution)/shard_map/hqk,kd->qhd/dot_general | solution.py:88
  65.6 0.1 copy.53
  65.8 2.5 %fusion.25 = bf16[64,8,256]{2,0,1:T(8,128)(2,1)} fusion(bf16[8,256,384]{1,2,0:T(8,128)(2,1)} %copy-done.3, bf16[256,256]{0,1:T(8,128)(2,1)S(1)} %bitcast.211, bf16[128,256]{0,1:T(8,128)(2,1)S(1)} %collective-permute-done), kind=kOutput, calls=%fused_computation.46 | convolution fusion | flops 101023744 | bytes 2031616 | tf_op jit(solution)/shard_map/hqk,kd->qhd/dot_general | solution.py:88
  68.3 1.1 copy.52
  69.4 1.2 fusion.27
  70.6 0.1 copy.54
  70.8 60.4 %reduce-scatter.4.cloned.1.call-done = f32[192,256]{1,0:T(8,128)} async-done(((f32[1536,256]{1,0:T(8,128)}), f32[192,256]{1,0:T(8,128)}) %reduce-scatter.4.cloned.1.call-update) | async-done | bytes 196624
  131.2 1.8 %copy.69 = f32[192,256]{0,1:T(8,128)} copy(f32[192,256]{1,0:T(8,128)} %reduce-scatter.4.cloned.1.call-done) | data formatting | bytes 393216
  133.0 1.1 maximum_bitcast_fusion
  134.1 30.6 %all-reduce.2.cloned.1.call-done = f32[192,256]{0,1:T(8,128)} async-done(((f32[192,256]{0,1:T(8,128)}), f32[192,256]{0,1:T(8,128)}) %all-reduce.2.cloned.1.call-update) | async-done | bytes 196624 | tf_op jit(solution)/shard_map/psum | solution.py:111
  164.7 1.7 %copy.59 = f32[192,256]{1,0:T(8,128)} copy(f32[192,256]{0,1:T(8,128)} %all-reduce.2.cloned.1.call-done) | data formatting | bytes 393216
  (47 shorter events, 0.6 us)
Async XLA Ops:
  7.2 51.4 %copy-start = (bf16[1,256,1536]{2,1,0:T(8,128)(2,1)S(1)}, bf16[1,256,1536]{2,1,0:T(8,128)(2,1)}, u32[]{:S(2)}) copy-start(bf16[1,256,1536]{2,1,0:T(8,128)(2,1)} %param.12) | copy-start | bytes 2359300
  7.2 19.7 %copy-start.8 = (bf16[1,256,2048]{2,1,0:T(8,128)(2,1)S(1)}, bf16[1,256,2048]{2,1,0:T(8,128)(2,1)}, u32[]{:S(2)}) copy-start(bf16[1,256,2048]{2,1,0:T(8,128)(2,1)} %param.11) | copy-start | bytes 3145732
  7.2 124.0 %reduce-scatter.4.cloned.1.call-start = ((), (), s32[]{:S(2)}) async-start(), calls=%async_computation.2 | async-start | bytes 1769472
  8.6 24.6 %collective-permute-start.1 = (bf16[128]{0:T(256)(128)(2,1)}, bf16[128]{0:T(256)(128)(2,1)}, u32[]{:S(2)}, u32[]{:S(2)}) collective-permute-start(bf16[128]{0:T(256)(128)(2,1)} %slice.98), channel_id=1, source_target_pairs={{0,1},{1,2},{2,3},{4,5},{5,6},{6,7},{8,9},{9,10},{10,11},{12,13},{... | collective-permute-start | bytes 776 | tf_op jit(solution)/shard_map/ppermute | solution.py:15
  13.2 21.6 %collective-permute-start = (bf16[128,256]{0,1:T(8,128)(2,1)}, bf16[128,256]{0,1:T(8,128)(2,1)S(1)}, u32[]{:S(2)}, u32[]{:S(2)}) collective-permute-start(bf16[128,256]{0,1:T(8,128)(2,1)} %slice_bitcast_fusion.1), channel_id=1, source_target_pairs={{0,1},{1,2},{2,3},{4,5},{5,6},{6,7},{8,9},{9,10},{10,11},{12,13},{... | collective-permute-start | bytes 196616 | tf_op jit(solution)/shard_map/ppermute | solution.py:15
  18.8 19.3 %collective-permute-start.2 = (bf16[128,256]{0,1:T(8,128)(2,1)}, bf16[128,256]{0,1:T(8,128)(2,1)S(1)}, u32[]{:S(2)}, u32[]{:S(2)}) collective-permute-start(bf16[128,256]{0,1:T(8,128)(2,1)} %slice_bitcast_fusion), channel_id=1, source_target_pairs={{0,1},{1,2},{2,3},{4,5},{5,6},{6,7},{8,9},{9,10},{10,11},{12,13},{... | collective-permute-start | bytes 196616 | tf_op jit(solution)/shard_map/ppermute | solution.py:15
  26.4 8.9 %copy-start.5 = (bf16[256,512]{0,1:T(8,128)(2,1)}, bf16[256,512]{0,1:T(8,128)(2,1)S(1)}, u32[]{:S(2)}) copy-start(bf16[256,512]{0,1:T(8,128)(2,1)S(1)} %copy.48) | copy-start | bytes 786436
  34.8 1.3 copy-start.9
  34.8 1.3 copy-start.12
  40.7 2.8 %copy-start.11 = (bf16[256,512]{0,1:T(8,128)(2,1)S(1)}, bf16[256,512]{0,1:T(8,128)(2,1)}, u32[]{:S(2)}) copy-start(bf16[256,512]{0,1:T(8,128)(2,1)} %copy.43) | copy-start | bytes 786436
  43.5 2.9 %copy-start.7 = (bf16[256,512]{0,1:T(8,128)(2,1)S(1)}, bf16[256,512]{0,1:T(8,128)(2,1)}, u32[]{:S(2)}) copy-start(bf16[256,512]{0,1:T(8,128)(2,1)} %copy.49) | copy-start | bytes 786436
  46.3 1.0 copy-start.10
  49.5 4.3 %copy-start.6 = (bf16[256,512]{0,1:T(8,128)(2,1)S(1)}, bf16[256,512]{0,1:T(8,128)(2,1)}, u32[]{:S(2)}) copy-start(bf16[256,512]{0,1:T(8,128)(2,1)} %copy-done.5) | copy-start | bytes 786436
  53.1 1.9 %copy-start.1 = (bf16[8,256,384]{1,2,0:T(8,128)(2,1)}, bf16[8,256,384]{1,2,0:T(8,128)(2,1)S(1)}, u32[]{:S(2)}) copy-start(bf16[8,256,384]{1,2,0:T(8,128)(2,1)S(1)} %get-tuple-element.32) | copy-start | bytes 4718596
  53.1 1.9 %copy-start.3 = (bf16[8,256,384]{1,2,0:T(8,128)(2,1)}, bf16[8,256,384]{1,2,0:T(8,128)(2,1)S(1)}, u32[]{:S(2)}) copy-start(bf16[8,256,384]{1,2,0:T(8,128)(2,1)S(1)} %get-tuple-element.31) | copy-start | bytes 4718596
  53.1 2.1 %copy-start.4 = (bf16[8,256,384]{1,2,0:T(8,128)(2,1)}, bf16[8,256,384]{1,2,0:T(8,128)(2,1)S(1)}, u32[]{:S(2)}) copy-start(bf16[8,256,384]{1,2,0:T(8,128)(2,1)S(1)} %get-tuple-element.33) | copy-start | bytes 4718596
  53.2 3.4 %copy-start.13 = (f32[1,256]{1,0:T(1,128)S(1)}, f32[1,256]{1,0:T(1,128)}, u32[]{:S(2)}) copy-start(f32[1,256]{1,0:T(1,128)} %convert_element_type.102) | copy-start | bytes 3076
  53.2 3.4 %copy-start.14 = (f32[32]{0:T(128)S(1)}, f32[32]{0:T(128)}, u32[]{:S(2)}) copy-start(f32[32]{0:T(128)} %negate_power_fusion) | copy-start | bytes 388
  55.3 3.1 %collective-permute-start.3 = (bf16[128,256]{0,1:T(8,128)(2,1)S(1)}, bf16[128,256]{0,1:T(8,128)(2,1)S(1)}, u32[]{:S(2)}, u32[]{:S(2)}) collective-permute-start(bf16[128,256]{0,1:T(8,128)(2,1)S(1)} %slice.226), channel_id=1, source_target_pairs={{1,0},{2,1},{3,2},{5,4},{6,5},{7,6},{9,8},{10,9},{11,10},{13,12},{... | collective-permute-start | bytes 196616 | tf_op jit(solution)/shard_map/ppermute | solution.py:15
  63.1 101.5 %all-reduce.2.cloned.1.call-start = ((), (), s32[]{:S(2)}) async-start(), calls=%async_computation.1 | async-start | bytes 524288 | tf_op jit(solution)/shard_map/psum | solution.py:111
  63.6 5.8 %copy-start.2 = (bf16[8,256,384]{1,2,0:T(8,128)(2,1)S(1)}, bf16[8,256,384]{1,2,0:T(8,128)(2,1)}, u32[]{:S(2)}) copy-start(bf16[8,256,384]{1,2,0:T(8,128)(2,1)} %copy-done.1) | copy-start | bytes 4718596
Sparse Core Ops, SparseCore 0:
  63.3 67.8 reduce-scatter.3
  133.5 31.1 all-reduce.1
where the time goes:
time: 174 us; the launch traced here: 173 us
  waiting for transfers between devices  92.7 us (53%)
  local copies, waits for them, and re-layouts  22 us (13%)
  matrix products  20.4 us (12%)
  between operations  14.5 us (8%)
  other arithmetic  13.5 us (8%)
  starting transfers between devices  10.2 us (6%)
    unnamed x3, waiting for transfers between devices  60.4 us
    psum x1, waiting for transfers between devices, body(): shard = lax.psum(shard, 'seq')  30.6 us
    ppermute x4, starting transfers between devices, from_behind(): return lax.ppermute(shard, axis, pairs)  10.1 us
    unnamed x35, local copies, waits for them, and re-layouts  9.09 us
    dot_general x4, matrix products, body(): jnp.einsum('qhd,kd->hqk', g_grp, v_grp, preferred_element_type=jnp.float32)  8.07 us
    slice x5, local copies, waits for them, and re-layouts, body(): g_grp = grad_out[:, low_col:high_col].reshape(tok_rows, group, head_dim)  6.38 us
    dot_general x4, matrix products, body(): jnp.einsum('hqk,kd->qhd', grad_b, k_grp, preferred_element_type=jnp.float32)  6.01 us
    convert_element_type x2, other arithmetic, body(): grad_b = grad_scores.astype(jnp.bfloat16)  5.62 us
  transfers between devices with their start and end apart: 6, of which 3 were waited for; matrix products, arithmetic and copies ran while one was open for 17% of the time, Pallas kernels for 0%

commit v1 on v0

--- a/solution.py
+++ b/solution.py
@@ -108,7 +108,7 @@
         scatter_dimension=0,
         tiled=True,
     )
-    shard = lax.psum(shard, "seq")
+    shard = jnp.sum(lax.all_gather(shard, "seq"), axis=0)
     return (grad_query[None], shard)
 
 

time: 174 us -> 148 us (0.85)
  waiting for transfers between devices: 92.7 us -> 61 us
  blocking collectives: 0 us -> 8.78 us
  local copies, waits for them, and re-layouts: 22 us -> 18.5 us
    unnamed x3 -> x1, waiting for transfers between devices: 60.4 us -> 0.02 us
    reduce_scatter x0 -> x1, waiting for transfers between devices: none -> 59.4 us  [body(): lax.psum_scatter(lax.dot_general(layer_input, k_grads, (((0,), (0,)), (()...]
    psum x1 -> x0, waiting for transfers between devices: 30.6 us -> none  [body(): shard = lax.psum(shard, 'seq')]
    all_gather x0 -> x1, blocking collectives: none -> 8.78 us  [body(): shard = jnp.sum(lax.all_gather(shard, 'seq'), axis=0)]
    unnamed x35 -> x33, local copies, waits for them, and re-layouts: 9.09 us -> 5.59 us
  transfers between devices with their start and end apart: 6 -> 5, of which waited for: 3 -> 2; matrix products, arithmetic and copies ran while one was open for 17% -> 20% of each run, Pallas kernels for 0% -> 0%
where the time goes in v1:
time: 148 us
  waiting for transfers between devices  61 us (41%)
  matrix products  20.4 us (14%)
  local copies, waits for them, and re-layouts  18.5 us (12%)
  between operations  14.5 us (10%)
  other arithmetic  14.3 us (10%)
  starting transfers between devices  10.2 us (7%)
  blocking collectives  8.78 us (6%)
    reduce_scatter x1, waiting for transfers between devices, body(): lax.psum_scatter(lax.dot_general(layer_input, k_grads, (((0,), (0,)), (()...  59.4 us
    ppermute x4, starting transfers between devices, from_behind(): return lax.ppermute(shard, axis, pairs)  10.1 us
    all_gather x1, blocking collectives, body(): shard = jnp.sum(lax.all_gather(shard, 'seq'), axis=0)  8.78 us
    dot_general x4, matrix products, body(): jnp.einsum('qhd,kd->hqk', g_grp, v_grp, preferred_element_type=jnp.float32)  8.07 us
    slice x5, local copies, waits for them, and re-layouts, body(): g_grp = grad_out[:, low_col:high_col].reshape(tok_rows, group, head_dim)  6.38 us
    dot_general x4, matrix products, body(): jnp.einsum('hqk,kd->qhd', grad_b, k_grp, preferred_element_type=jnp.float32)  6.01 us
    convert_element_type x2, other arithmetic, body(): grad_b = grad_scores.astype(jnp.bfloat16)  5.62 us
    unnamed x33, local copies, waits for them, and re-layouts  5.59 us
  transfers between devices with their start and end apart: 5, of which 2 were waited for; matrix products, arithmetic and copies ran while one was open for 20% of the time, Pallas kernels for 0%

profile of v1, /device:TPU:0, one launch (start us, length us, event | category | flops | bytes accessed | tf_op | source)
XLA Modules:
  0.0 147.5 jit_solution(1178555032579489738)
XLA Ops:
  7.2 0.8 fusion.83
  8.0 0.6 slice.98
  8.6 2.9 %collective-permute-start.1 = (bf16[128]{0:T(256)(128)(2,1)}, bf16[128]{0:T(256)(128)(2,1)}, u32[]{:S(2)}, u32[]{:S(2)}) collective-permute-start(bf16[128]{0:T(256)(128)(2,1)} %slice.98), channel_id=1, source_target_pairs={{0,1},{1,2},{2,3},{4,5},{5,6},{6,7},{8,9},{9,10},{10,11},{12,13},{... | collective-permute-start | bytes 776 | tf_op jit(solution)/shard_map/ppermute | solution.py:15
  11.5 1.0 copy.59
  12.5 0.6 slice_bitcast_fusion.1
  13.2 4.0 %collective-permute-start = (bf16[128,256]{0,1:T(8,128)(2,1)}, bf16[128,256]{0,1:T(8,128)(2,1)S(1)}, u32[]{:S(2)}, u32[]{:S(2)}) collective-permute-start(bf16[128,256]{0,1:T(8,128)(2,1)} %slice_bitcast_fusion.1), channel_id=1, source_target_pairs={{0,1},{1,2},{2,3},{4,5},{5,6},{6,7},{8,9},{9,10},{10,11},{12,13},{... | collective-permute-start | bytes 196616 | tf_op jit(solution)/shard_map/ppermute | solution.py:15
  17.2 1.0 copy.62
  18.2 0.6 slice_bitcast_fusion
  18.8 1.9 %collective-permute-start.2 = (bf16[128,256]{0,1:T(8,128)(2,1)}, bf16[128,256]{0,1:T(8,128)(2,1)S(1)}, u32[]{:S(2)}, u32[]{:S(2)}) collective-permute-start(bf16[128,256]{0,1:T(8,128)(2,1)} %slice_bitcast_fusion), channel_id=1, source_target_pairs={{0,1},{1,2},{2,3},{4,5},{5,6},{6,7},{8,9},{9,10},{10,11},{12,13},{... | collective-permute-start | bytes 196616 | tf_op jit(solution)/shard_map/ppermute | solution.py:15
  20.7 0.6 negate_power_fusion
  21.3 0.5 iota_add_fusion
  21.9 0.6 fusion.70
  22.4 1.2 convert_element_type.102
  23.7 1.3 fusion.88
  25.0 1.3 fusion.85
  26.3 0.1 copy.72
  26.4 0.1 copy.69
  26.6 0.1 copy.66
  26.7 0.1 copy.61
  26.9 0.9 fusion.86
  27.8 1.1 copy.64
  28.8 1.8 %copy.73 = bf16[256,512]{0,1:T(8,128)(2,1)} copy(bf16[256,512]{1,0:T(8,128)(2,1)} %get-tuple-element.18) | data formatting | bytes 524288 | tf_op jit(solution)/shard_map/slice | solution.py:73
  30.6 1.8 %copy.70 = bf16[256,512]{0,1:T(8,128)(2,1)} copy(bf16[256,512]{1,0:T(8,128)(2,1)} %get-tuple-element.19) | data formatting | bytes 524288 | tf_op jit(solution)/shard_map/slice | solution.py:73
  32.4 0.8 copy.67
  33.3 0.6 convert_element_type.84
  33.9 0.9 fusion.37
  34.8 0.6 fusion.89
  35.4 0.7 fusion.12
  36.0 0.1 broadcast_maximum_fusion.3
  36.1 0.8 fusion.17
  36.9 0.6 fusion.62
  37.5 0.6 fusion.68
  38.1 0.1 exponential_add_fusion.3
  38.1 2.5 %fusion.9 = (f32[8,256]{1,0:T(8,128)S(1)}, f32[8,256]{1,0:T(8,128)S(1)}, f32[8,256]{1,0:T(8,128)S(1)}, f32[8,256]{1,0:T(8,128)S(1)}, f32[384,256,8]{1,0,2:T(8,128)S(1)}) fusion(f32[8,256]{1,0:T(8,128)S(1)} %exponential_add_fusion.3, f32[8,256]{1,0:T(8,128)S(1)} %broadcast_maximum_fusion.3, f32[384,256,8]{1,0,2:T(8,128)S(1)} %get-tuple-element.37, ...), kind=kOutput, calls=%fused_computation.20 | convolution fusion | flops 113336320 | bytes 16334848 | tf_op jit(solution)/shard_map/qhd,kd->hqk/dot_general | solution.py:83
  40.7 2.0 %fusion.11 = (bf16[8,256,384]{1,2,0:T(8,128)(2,1)S(1)}, f32[8,256]{1,0:T(8,128)S(1)}) fusion(f32[384,256,8]{1,0,2:T(8,128)S(1)} %get-tuple-element.38, f32[8,256]{1,0:T(8,128)S(1)} %get-tuple-element.2, f32[8,256]{1,0:T(8,128)S(1)} %exponential_add_fusion.3, f32[8,256]{1,0:T(8,128)S(1)} %broadcast_maximum_fusion.3, f32[384,256,8]{1,0,2:T(8,128)S(1)} %get-tuple-element.37, ...), kind=kLoop, calls=%fused_computation.22 | loop fusion | flops 10221568 | bytes 11149312 | tf_op jit(solution)/shard_map/convert_element_type | solution.py:86
  42.7 0.6 fusion.31
  43.3 0.1 exponential_add_fusion.2
  43.5 2.8 %fusion.6 = (f32[8,256]{1,0:T(8,128)S(1)}, f32[8,256]{1,0:T(8,128)S(1)}, f32[8,256]{1,0:T(8,128)S(1)}, f32[384,256,8]{1,0,2:T(8,128)S(1)}) fusion(f32[8,256]{1,0:T(8,128)S(1)} %exponential_add_fusion.2, f32[8,256]{1,0:T(8,128)S(1)} %broadcast_maximum_fusion.2, f32[384,256,8]{1,0,2:T(8,128)S(1)} %fusion.62, pred[256,384]{0,1:T(8,128)(4,1)S(1)} %fusion.37, ...), kind=kOutput, calls=%fused_computation.14 | convolution fusion | flops 114124800 | bytes 13197312 | tf_op jit(solution)/shard_map/qhd,kd->hqk/dot_general | solution.py:83
  46.3 0.1 exponential_add_fusion
  46.4 0.6 fusion.57
  47.0 0.3 copy-done.10
  47.2 2.2 %fusion.3 = (f32[8,256]{1,0:T(8,128)S(1)}, f32[8,256]{1,0:T(8,128)S(1)}, f32[384,256,8]{1,0,2:T(8,128)S(1)}) fusion(f32[8,256]{1,0:T(8,128)S(1)} %get-tuple-element.42, f32[8,256]{1,0:T(8,128)S(1)} %broadcast_maximum_fusion.1, f32[384,256,8]{1,0,2:T(8,128)S(1)} %fusion.68, pred[256,384]{0,1:T(8,128)(4,1)S(1)} %fusion.37, f32[384,256,8]{1,0,2:T(8,128)S(1)} %fusion.57, ...), kind=kOutput, calls=%fused_computation.8 | convolution fusion | flops 111767552 | bytes 13189120 | tf_op jit(solution)/shard_map/qhd,kd->hqk/dot_general | solution.py:83
  49.5 3.6 %fusion.8 = (bf16[8,256,384]{1,2,0:T(8,128)(2,1)S(1)}, bf16[8,256,384]{1,2,0:T(8,128)(2,1)S(1)}, bf16[8,256,384]{1,2,0:T(8,128)(2,1)S(1)}) fusion(f32[384,256,8]{1,0,2:T(8,128)S(1)} %get-tuple-element.39, f32[8,256]{1,0:T(8,128)S(1)} %get-tuple-element.6, f32[8,256]{1,0:T(8,128)S(1)} %exponential_add_fusion.2, f32[8,256]{1,0:T(8,128)S(1)} %broadcast_maximum_fusion.2, ...), kind=kLoop, calls=%fused_computation.16 | loop fusion | flops 18874368 | bytes 23764992 | tf_op jit(solution)/shard_map/convert_element_type | solution.py:86
  53.2 0.6 fusion.29
  53.8 0.6 fusion.28
  54.4 0.6 fusion.30
  55.0 0.2 copy-done.4
  55.3 1.3 collective-permute-start.3
  56.6 0.2 multiply_cosine_fusion
  56.8 1.6 %collective-permute-done.3 = bf16[128,256]{0,1:T(8,128)(2,1)S(1)} collective-permute-done((bf16[128,256]{0,1:T(8,128)(2,1)S(1)}, bf16[128,256]{0,1:T(8,128)(2,1)S(1)}, u32[]{:S(2)}, u32[]{:S(2)}) %collective-permute-start.3) | collective-permute-done | bytes 65568 | tf_op jit(solution)/shard_map/ppermute | solution.py:15
  58.5 1.5 %convolution_bitcast_fusion = f32[1536,256]{0,1:T(8,128)} fusion(bf16[256,256]{0,1:T(8,128)(2,1)S(1)} %bitcast.234, bf16[1,256,1536]{2,1,0:T(8,128)(2,1)S(1)} %copy-done), kind=kOutput, calls=%fused_computation.32 | convolution fusion | flops 201326592 | bytes 2490368 | tf_op jit(solution)/shard_map/dot_general | solution.py:104
  60.1 3.1 %copy.92 = f32[1536,256]{1,0:T(8,128)} copy(f32[1536,256]{0,1:T(8,128)} %convolution_bitcast_fusion) | data formatting | bytes 3145728
  63.1 0.4 fusion.24
  63.6 0.1 copy.75
  63.7 1.9 %fusion.26 = bf16[64,8,256]{2,0,1:T(8,128)(2,1)S(1)} fusion(bf16[8,256,384]{1,2,0:T(8,128)(2,1)} %copy-done.4, bf16[256,256]{0,1:T(8,128)(2,1)S(1)} %bitcast.211, bf16[128,256]{0,1:T(8,128)(2,1)S(1)} %collective-permute-done), kind=kOutput, calls=%fused_computation.47 | convolution fusion | flops 101023744 | bytes 2031616 | tf_op jit(solution)/shard_map/hqk,kd->qhd/dot_general | solution.py:88
  65.6 0.1 copy.77
  65.7 2.5 %fusion.25 = bf16[64,8,256]{2,0,1:T(8,128)(2,1)} fusion(bf16[8,256,384]{1,2,0:T(8,128)(2,1)} %copy-done.3, bf16[256,256]{0,1:T(8,128)(2,1)S(1)} %bitcast.212, bf16[128,256]{0,1:T(8,128)(2,1)S(1)} %collective-permute-done), kind=kOutput, calls=%fused_computation.46 | convolution fusion | flops 101023744 | bytes 2031616 | tf_op jit(solution)/shard_map/hqk,kd->qhd/dot_general | solution.py:88
  68.3 1.1 copy.76
  69.4 1.2 fusion.27
  70.6 0.1 copy.78
  70.7 1.1 maximum_bitcast_fusion
  71.8 59.4 %reduce-scatter.4.cloned.1.call-done = f32[192,256]{1,0:T(8,128)} async-done(((f32[1536,256]{1,0:T(8,128)}), f32[192,256]{1,0:T(8,128)}) %reduce-scatter.4.cloned.1.call-update) | async-done | bytes 196624 | tf_op jit(solution)/shard_map/reduce_scatter | solution.py:103
  131.2 8.8 %all-gather = f32[768,256]{1,0:T(8,128)S(1)} all-gather(f32[192,256]{1,0:T(8,128)} %reduce-scatter.4.cloned.1.call-done), channel_id=2, replica_groups=mesh['dp'=8,'seq'=4] {'seq'}, dimensions={0}, use_global_device_ids=true | all-gather | bytes 983040 | tf_op jit(solution)/shard_map/all_gather | solution.py:111
  140.0 0.7 reduce_sum.89
  (44 shorter events, 0.5 us)
Async XLA Ops:
  7.2 51.4 %copy-start = (bf16[1,256,1536]{2,1,0:T(8,128)(2,1)S(1)}, bf16[1,256,1536]{2,1,0:T(8,128)(2,1)}, u32[]{:S(2)}) copy-start(bf16[1,256,1536]{2,1,0:T(8,128)(2,1)} %param.12) | copy-start | bytes 2359300
  7.2 19.7 %copy-start.8 = (bf16[1,256,2048]{2,1,0:T(8,128)(2,1)S(1)}, bf16[1,256,2048]{2,1,0:T(8,128)(2,1)}, u32[]{:S(2)}) copy-start(bf16[1,256,2048]{2,1,0:T(8,128)(2,1)} %param.11) | copy-start | bytes 3145732
  7.2 124.0 %reduce-scatter.4.cloned.1.call-start = ((), (), s32[]{:S(2)}) async-start(), calls=%async_computation.1 | async-start | bytes 1769472 | tf_op jit(solution)/shard_map/reduce_scatter | solution.py:103
  8.6 24.6 %collective-permute-start.1 = (bf16[128]{0:T(256)(128)(2,1)}, bf16[128]{0:T(256)(128)(2,1)}, u32[]{:S(2)}, u32[]{:S(2)}) collective-permute-start(bf16[128]{0:T(256)(128)(2,1)} %slice.98), channel_id=1, source_target_pairs={{0,1},{1,2},{2,3},{4,5},{5,6},{6,7},{8,9},{9,10},{10,11},{12,13},{... | collective-permute-start | bytes 776 | tf_op jit(solution)/shard_map/ppermute | solution.py:15
  13.2 21.6 %collective-permute-start = (bf16[128,256]{0,1:T(8,128)(2,1)}, bf16[128,256]{0,1:T(8,128)(2,1)S(1)}, u32[]{:S(2)}, u32[]{:S(2)}) collective-permute-start(bf16[128,256]{0,1:T(8,128)(2,1)} %slice_bitcast_fusion.1), channel_id=1, source_target_pairs={{0,1},{1,2},{2,3},{4,5},{5,6},{6,7},{8,9},{9,10},{10,11},{12,13},{... | collective-permute-start | bytes 196616 | tf_op jit(solution)/shard_map/ppermute | solution.py:15
  18.8 19.3 %collective-permute-start.2 = (bf16[128,256]{0,1:T(8,128)(2,1)}, bf16[128,256]{0,1:T(8,128)(2,1)S(1)}, u32[]{:S(2)}, u32[]{:S(2)}) collective-permute-start(bf16[128,256]{0,1:T(8,128)(2,1)} %slice_bitcast_fusion), channel_id=1, source_target_pairs={{0,1},{1,2},{2,3},{4,5},{5,6},{6,7},{8,9},{9,10},{10,11},{12,13},{... | collective-permute-start | bytes 196616 | tf_op jit(solution)/shard_map/ppermute | solution.py:15
  26.4 8.9 %copy-start.5 = (bf16[256,512]{0,1:T(8,128)(2,1)}, bf16[256,512]{0,1:T(8,128)(2,1)S(1)}, u32[]{:S(2)}) copy-start(bf16[256,512]{0,1:T(8,128)(2,1)S(1)} %copy.72) | copy-start | bytes 786436
  34.8 1.3 copy-start.9
  34.8 1.3 copy-start.12
  40.7 2.8 %copy-start.11 = (bf16[256,512]{0,1:T(8,128)(2,1)S(1)}, bf16[256,512]{0,1:T(8,128)(2,1)}, u32[]{:S(2)}) copy-start(bf16[256,512]{0,1:T(8,128)(2,1)} %copy.67) | copy-start | bytes 786436
  43.5 2.9 %copy-start.7 = (bf16[256,512]{0,1:T(8,128)(2,1)S(1)}, bf16[256,512]{0,1:T(8,128)(2,1)}, u32[]{:S(2)}) copy-start(bf16[256,512]{0,1:T(8,128)(2,1)} %copy.73) | copy-start | bytes 786436
  46.3 1.0 copy-start.10
  49.5 4.3 %copy-start.6 = (bf16[256,512]{0,1:T(8,128)(2,1)S(1)}, bf16[256,512]{0,1:T(8,128)(2,1)}, u32[]{:S(2)}) copy-start(bf16[256,512]{0,1:T(8,128)(2,1)} %copy-done.5) | copy-start | bytes 786436
  53.1 1.9 %copy-start.1 = (bf16[8,256,384]{1,2,0:T(8,128)(2,1)}, bf16[8,256,384]{1,2,0:T(8,128)(2,1)S(1)}, u32[]{:S(2)}) copy-start(bf16[8,256,384]{1,2,0:T(8,128)(2,1)S(1)} %get-tuple-element.28) | copy-start | bytes 4718596
  53.1 1.9 %copy-start.3 = (bf16[8,256,384]{1,2,0:T(8,128)(2,1)}, bf16[8,256,384]{1,2,0:T(8,128)(2,1)S(1)}, u32[]{:S(2)}) copy-start(bf16[8,256,384]{1,2,0:T(8,128)(2,1)S(1)} %get-tuple-element.27) | copy-start | bytes 4718596
  53.1 2.1 %copy-start.4 = (bf16[8,256,384]{1,2,0:T(8,128)(2,1)}, bf16[8,256,384]{1,2,0:T(8,128)(2,1)S(1)}, u32[]{:S(2)}) copy-start(bf16[8,256,384]{1,2,0:T(8,128)(2,1)S(1)} %get-tuple-element.29) | copy-start | bytes 4718596
  53.2 3.4 %copy-start.13 = (f32[1,256]{1,0:T(1,128)S(1)}, f32[1,256]{1,0:T(1,128)}, u32[]{:S(2)}) copy-start(f32[1,256]{1,0:T(1,128)} %convert_element_type.102) | copy-start | bytes 3076
  53.2 3.4 %copy-start.14 = (f32[32]{0:T(128)S(1)}, f32[32]{0:T(128)}, u32[]{:S(2)}) copy-start(f32[32]{0:T(128)} %negate_power_fusion) | copy-start | bytes 388
  55.3 3.1 %collective-permute-start.3 = (bf16[128,256]{0,1:T(8,128)(2,1)S(1)}, bf16[128,256]{0,1:T(8,128)(2,1)S(1)}, u32[]{:S(2)}, u32[]{:S(2)}) collective-permute-start(bf16[128,256]{0,1:T(8,128)(2,1)S(1)} %slice.226), channel_id=1, source_target_pairs={{1,0},{2,1},{3,2},{5,4},{6,5},{7,6},{9,8},{10,9},{11,10},{13,12},{... | collective-permute-start | bytes 196616 | tf_op jit(solution)/shard_map/ppermute | solution.py:15
  63.5 5.8 %copy-start.2 = (bf16[8,256,384]{1,2,0:T(8,128)(2,1)S(1)}, bf16[8,256,384]{1,2,0:T(8,128)(2,1)}, u32[]{:S(2)}) copy-start(bf16[8,256,384]{1,2,0:T(8,128)(2,1)} %copy-done.1) | copy-start | bytes 4718596
Sparse Core Ops, SparseCore 0:
  63.3 67.8 reduce-scatter.3
